TPU v7x, 32 devices: a whole 2x2x4 slice. The times are simulated.
32 devices in a mesh: groups: 2 (over y), seq: 8 (over z, x), chan: 2 (over core).
Axes of the slice: x: 2, y: 2, z: 4, core: 2. Of those that a mesh axis runs over, the one named last changes fastest.
Arguments:
- projected: bfloat16 [3, 2048, 1024], P(None, ('groups', 'seq'), 'chan'), parts along dimension 1, may hold values from -6 to 6
- long_filter: float32 [2048, 1024], P(('groups', 'seq'), 'chan'), parts along dimension 0, may hold values from -6 to 6
- short_kernel: float32 [3, 7, 1024], P(None, None, 'chan'), may hold values from -2 to 2
- skip_gain: float32 [1024], P('chan'), may hold values from 0.25 to 1.5
- cotangent: bfloat16 [2048, 1024], P(('groups', 'seq'), 'chan'), parts along dimension 0, may hold values from -6 to 6
Outputs:
- layer_output: bfloat16 [2048, 1024], P(('groups', 'seq'), 'chan'), parts along dimension 0
- stream_grads: bfloat16 [3, 2048, 1024], P(None, ('groups', 'seq'), 'chan'), parts along dimension 1
- filter_grad: float32 [2048, 1024], P(('groups', 'seq'), 'chan'), parts along dimension 0
- kernel_grad: float32 [6, 7, 1024], P('groups', None, 'chan'), parts along dimension 0
- skip_grad: float32 [2048], P(('groups', 'chan')), parts along dimension 0
There are 2 independent parts, one for each index of `groups`. A program takes and returns all parts, laid end to end along the dimension named above; an argument that names none is the same for every part. Nothing has to cross between parts.
All inputs are finite; a program needn't handle non-finite values.
Results may differ from a plain program's by a relative error of at most 0.001.
Values may be sent and summed in bfloat16 or wider, within the bound.
A program may use at most 64 MiB of HBM per device.

v0:
```python
import math

import jax
import jax.numpy as jnp
from jax import lax
from jax.sharding import PartitionSpec as P

HIGHEST = lax.Precision.HIGHEST


def with_halo(block, sides, width):
    for axis, dim in sides:
        count = lax.axis_size(axis)
        forward = [(i, i + 1) for i in range(count - 1)]
        forward.append((count - 1, 0))
        backward = [(target, source) for source, target in forward]
        low = lax.ppermute(
            lax.slice_in_dim(block, block.shape[dim] - width, None, axis=dim), axis, forward
        )
        high = lax.ppermute(lax.slice_in_dim(block, 0, width, axis=dim), axis, backward)
        block = jnp.concatenate([low, block, high], axis=dim)
    return block


def dft_tables(extent):
    indices = jnp.arange(extent, dtype=jnp.int32)
    angles = (indices[:, None] * indices[None, :] % extent).astype(jnp.float32) * (
        2.0 * math.pi / extent
    )
    return (jnp.cos(angles), jnp.sin(angles))


def apply_along(matrix, signal, axis_dim):
    letters = "wxyz"
    target = letters[:axis_dim] + "k" + letters[axis_dim + 1 :]
    return jnp.einsum(
        "k" + letters[axis_dim] + "," + letters + "->" + target, matrix, signal, precision=HIGHEST
    )


def forward_section(real_part, imaginary, axis_dim):
    cosine, sine_table = dft_tables(real_part.shape[axis_dim])
    out_real = apply_along(cosine, real_part, axis_dim)
    out_imag = -apply_along(sine_table, real_part, axis_dim)
    if imaginary is not None:
        out_real = out_real + apply_along(sine_table, imaginary, axis_dim)
        out_imag = out_imag + apply_along(cosine, imaginary, axis_dim)
    return (out_real, out_imag)


def inverse_section(real_part, imaginary, axis_dim, keep_imag):
    cosine, sine_table = dft_tables(real_part.shape[axis_dim])
    out_real = apply_along(cosine, real_part, axis_dim) - apply_along(
        sine_table, imaginary, axis_dim
    )
    if keep_imag:
        return (
            out_real,
            apply_along(sine_table, real_part, axis_dim) + apply_along(cosine, imaginary, axis_dim),
        )
    return (out_real, None)


def twist(real_part, imaginary, angles, sign_factor):
    cosine = jnp.cos(angles)
    sine_table = jnp.sin(angles)
    return (
        real_part * cosine + sign_factor * imaginary * sine_table,
        imaginary * cosine - sign_factor * real_part * sine_table,
    )


def twiddle(low_index, high_index, extent):
    return (low_index * high_index % extent).astype(jnp.float32) * (2.0 * math.pi / extent)


def block_angles(devices, portion, extent):
    low_index = jnp.arange(devices, dtype=jnp.int32)[None, :, None, None]
    high_index = (lax.axis_index("seq") * portion + jnp.arange(portion, dtype=jnp.int32))[
        None, None, :, None
    ]
    return twiddle(low_index, high_index, extent)


def sequence_forward(signals, extent):
    devices = lax.axis_size("seq")
    portion = signals.shape[1] // devices
    columns = lax.all_to_all(signals[:, None], "seq", split_axis=2, concat_axis=1, tiled=True)
    real_part, imaginary = forward_section(columns, None, 1)
    real_part, imaginary = twist(real_part, imaginary, block_angles(devices, portion, extent), 1.0)
    spread = (
        lax.all_to_all(real_part, "seq", split_axis=1, concat_axis=2, tiled=True),
        lax.all_to_all(imaginary, "seq", split_axis=1, concat_axis=2, tiled=True),
    )
    return forward_section(spread[0], spread[1], 2)


def sequence_inverse(real_part, imaginary, extent):
    devices = lax.axis_size("seq")
    portion = real_part.shape[2] // devices
    real_part, imaginary = inverse_section(real_part, imaginary, 2, True)
    gathered = (
        lax.all_to_all(real_part, "seq", split_axis=2, concat_axis=1, tiled=True),
        lax.all_to_all(imaginary, "seq", split_axis=2, concat_axis=1, tiled=True),
    )
    real_part, imaginary = twist(
        gathered[0], gathered[1], block_angles(devices, portion, extent), -1.0
    )
    pieces = inverse_section(real_part, imaginary, 1, False)[0] * (1.0 / extent)
    blocks = lax.all_to_all(pieces, "seq", split_axis=1, concat_axis=2, tiled=True)
    return blocks[:, 0]


def body(projected, long_filter, short_kernel, skip_gain, cotangent):
    rows_here = projected.shape[1]
    extent = rows_here * lax.axis_size("seq")
    factor = 1.0 / math.sqrt(extent)
    kernel_span = short_kernel.shape[1]
    margin = kernel_span // 2
    padded = with_halo(projected, (("seq", 1),), margin)
    shorts = jnp.zeros(projected.shape, jnp.float32)
    for offset in range(kernel_span):
        shorts = shorts + short_kernel[:, offset][:, None, :] * padded[
            :, offset : offset + rows_here
        ].astype(jnp.float32)
    gated_signal = shorts[1] * shorts[2]
    transform, restore = (sequence_forward, sequence_inverse)
    upstream = cotangent.astype(jnp.float32)
    grad_response = upstream * shorts[0]
    spec_real, spec_imag = transform(jnp.stack([gated_signal, long_filter]), extent)
    gated_real, gated_imag = (spec_real[0], spec_imag[0])
    filter_real, filter_imag = (spec_real[1] * factor, spec_imag[1] * factor)
    product_real = filter_real * gated_real - filter_imag * gated_imag
    product_imag = filter_real * gated_imag + filter_imag * gated_real
    convolved = restore(product_real[None], product_imag[None], extent)[0]
    upstream_real, upstream_imag = transform(grad_response[None], extent)
    upstream_real, upstream_imag = (upstream_real[0], upstream_imag[0])
    back_real = jnp.stack(
        [
            filter_real * upstream_real + filter_imag * upstream_imag,
            gated_real * upstream_real + gated_imag * upstream_imag,
        ]
    )
    back_imag = jnp.stack(
        [
            filter_real * upstream_imag - filter_imag * upstream_real,
            gated_real * upstream_imag - gated_imag * upstream_real,
        ]
    )
    restored = restore(back_real, back_imag, extent)
    grad_gated = restored[0] + skip_gain * grad_response
    filter_grad = restored[1] * factor
    response = convolved + skip_gain * gated_signal
    layer_output = (response * shorts[0]).astype(jnp.bfloat16)
    grad_shorts = jnp.stack([upstream * response, grad_gated * shorts[2], grad_gated * shorts[1]])
    rimmed = with_halo(grad_shorts, (("seq", 1),), margin)
    stream_sum = jnp.zeros(grad_shorts.shape, jnp.float32)
    kernel_terms = []
    for offset in range(kernel_span):
        start_row = 2 * margin - offset
        stream_sum = (
            stream_sum
            + short_kernel[:, offset][:, None, :] * rimmed[:, start_row : start_row + rows_here]
        )
        kernel_terms.append(
            jnp.sum(
                grad_shorts * padded[:, offset : offset + rows_here].astype(jnp.float32), axis=1
            )
        )
    kernel_part = jnp.stack(kernel_terms, axis=1)
    skip_part = jnp.sum(grad_response * gated_signal, axis=0)
    kernel_total, skip_total = lax.psum((kernel_part, skip_part), "seq")
    return (
        layer_output,
        stream_sum.astype(jnp.bfloat16),
        filter_grad,
        kernel_total * factor,
        skip_total * factor,
    )


def solution(mesh):
    placed = (
        P(None, ("groups", "seq"), "chan"),
        P(("groups", "seq"), "chan"),
        P(None, None, "chan"),
        P("chan"),
        P(("groups", "seq"), "chan"),
    )
    return jax.shard_map(
        body,
        mesh=mesh,
        in_specs=placed,
        out_specs=(
            P(("groups", "seq"), "chan"),
            P(None, ("groups", "seq"), "chan"),
            P(("groups", "seq"), "chan"),
            P("groups", None, "chan"),
            P(("groups", "chan")),
        ),
        check_vma=False,
    )
```

profile of v0, /device:TPU:0, one launch (start us, length us, event | category | flops | bytes accessed | tf_op | source)
XLA Modules:
  0.0 248.4 jit_solution(6842409723577557810)
XLA Ops:
  1.4 6.0 %collective-permute-start.1 = (bf16[3,3,512]{2,1,0:T(4,128)(2,1)S(1)}, bf16[3,3,512]{2,1,0:T(4,128)(2,1)S(1)}, u32[]{:S(2)}, u32[]{:S(2)}) collective-permute-start(bf16[3,3,512]{2,1,0:T(4,128)(2,1)S(1)} %get-tuple-element.52), channel_id=1, source_target_pairs={{2,0},{4,2},{6,4},{8,6},{10,8},{12,10},{14,12},{0,14},{3,1},{5,3},... | collective-permute-start | bytes 27656 | tf_op jit(solution)/shard_map/ppermute | solution.py:20
  7.5 1.1 constant_dynamic-update-slice_fusion.1
  8.9 5.0 %collective-permute-done = bf16[3,3,512]{2,1,0:T(4,128)(2,1)S(1)} collective-permute-done((bf16[3,3,512]{2,1,0:T(4,128)(2,1)S(1)}, bf16[3,3,512]{2,1,0:T(4,128)(2,1)S(1)}, u32[]{:S(2)}, u32[]{:S(2)}) %collective-permute-start) | collective-permute-done | bytes 9248 | tf_op jit(solution)/shard_map/ppermute | solution.py:17
  15.8 3.4 %all-to-all-start.6 = ((f32[1,1,128,512]{3,1,0,2:T(1,128)}), f32[1,1,128,512]{3,1,0,2:T(1,128)S(1)}, u32[]{:S(2)}, u32[]{:S(2)}) async-start(f32[1,1,128,512]{3,1,0,2:T(1,128)} %copy.61), calls=%async_computation.6 | async-start | bytes 524288 | tf_op jit(solution)/shard_map/all_to_all | solution.py:88
  20.2 1.2 copy.42
  21.4 6.0 %all-to-all-done.6 = f32[1,1,128,512]{3,1,0,2:T(1,128)S(1)} async-done(((f32[1,1,128,512]{3,1,0,2:T(1,128)}), f32[1,1,128,512]{3,1,0,2:T(1,128)S(1)}, u32[]{:S(2)}, u32[]{:S(2)}) %all-to-all-start.6) | async-done | bytes 262176 | tf_op jit(solution)/shard_map/all_to_all | solution.py:88
  27.3 3.5 %all-to-all-start = ((f32[2,1,128,512]{3,0,1,2:T(2,128)}), f32[2,1,128,512]{3,0,1,2:T(2,128)S(1)}, u32[]{:S(2)}, u32[]{:S(2)}) async-start(f32[2,1,128,512]{3,0,1,2:T(2,128)} %copy.42), calls=%async_computation | async-start | bytes 1048576 | tf_op jit(solution)/shard_map/all_to_all | solution.py:88
  33.0 10.4 %all-to-all-done = f32[2,1,128,512]{3,0,1,2:T(2,128)S(1)} async-done(((f32[2,1,128,512]{3,0,1,2:T(2,128)}), f32[2,1,128,512]{3,0,1,2:T(2,128)S(1)}, u32[]{:S(2)}, u32[]{:S(2)}) %all-to-all-start) | async-done | bytes 524320 | tf_op jit(solution)/shard_map/all_to_all | solution.py:88
  43.4 3.6 %all-to-all-start.7 = ((f32[1,8,16,512]{3,2,0,1:T(8,128)}), f32[1,8,16,512]{3,2,0,1:T(8,128)S(1)}, u32[]{:S(2)}, u32[]{:S(2)}) async-start(f32[1,8,16,512]{3,2,0,1:T(8,128)} %copy.64), calls=%async_computation.7 | async-start | bytes 524288 | tf_op jit(solution)/shard_map/all_to_all | solution.py:92
  48.0 7.3 %all-to-all-done.7 = f32[1,8,16,512]{3,2,0,1:T(8,128)S(1)} async-done(((f32[1,8,16,512]{3,2,0,1:T(8,128)}), f32[1,8,16,512]{3,2,0,1:T(8,128)S(1)}, u32[]{:S(2)}, u32[]{:S(2)}) %all-to-all-start.7) | async-done | bytes 262176 | tf_op jit(solution)/shard_map/all_to_all | solution.py:92
  55.3 3.4 %all-to-all-start.8 = ((f32[1,8,16,512]{3,2,0,1:T(8,128)}), f32[1,8,16,512]{3,2,0,1:T(8,128)S(1)}, u32[]{:S(2)}, u32[]{:S(2)}) async-start(f32[1,8,16,512]{3,2,0,1:T(8,128)} %copy.65), calls=%async_computation.8 | async-start | bytes 524288 | tf_op jit(solution)/shard_map/all_to_all | solution.py:93
  59.6 1.0 multiply_add_fusion
  60.6 1.1 copy.49
  61.7 5.2 %all-to-all-done.8 = f32[1,8,16,512]{3,2,0,1:T(8,128)S(1)} async-done(((f32[1,8,16,512]{3,2,0,1:T(8,128)}), f32[1,8,16,512]{3,2,0,1:T(8,128)S(1)}, u32[]{:S(2)}, u32[]{:S(2)}) %all-to-all-start.8) | async-done | bytes 262176 | tf_op jit(solution)/shard_map/all_to_all | solution.py:93
  66.9 3.5 %all-to-all-start.2 = ((f32[2,8,16,512]{3,2,0,1:T(8,128)}), f32[2,8,16,512]{3,2,0,1:T(8,128)S(1)}, u32[]{:S(2)}, u32[]{:S(2)}) async-start(f32[2,8,16,512]{3,2,0,1:T(8,128)} %copy.49), calls=%async_computation.2 | async-start | bytes 1048576 | tf_op jit(solution)/shard_map/all_to_all | solution.py:93
  70.4 1.1 copy.46
  71.5 12.8 %all-to-all-done.2 = f32[2,8,16,512]{3,2,0,1:T(8,128)S(1)} async-done(((f32[2,8,16,512]{3,2,0,1:T(8,128)}), f32[2,8,16,512]{3,2,0,1:T(8,128)S(1)}, u32[]{:S(2)}, u32[]{:S(2)}) %all-to-all-start.2) | async-done | bytes 524320 | tf_op jit(solution)/shard_map/all_to_all | solution.py:93
  84.3 3.7 %all-to-all-start.1 = ((f32[2,8,16,512]{3,2,0,1:T(8,128)}), f32[2,8,16,512]{3,2,0,1:T(8,128)S(1)}, u32[]{:S(2)}, u32[]{:S(2)}) async-start(f32[2,8,16,512]{3,2,0,1:T(8,128)} %copy.46), calls=%async_computation.1 | async-start | bytes 1048576 | tf_op jit(solution)/shard_map/all_to_all | solution.py:92
  88.7 1.4 fusion.8
  90.2 1.4 fusion.92
  91.6 1.1 fusion.80
  92.8 9.4 %all-to-all-done.1 = f32[2,8,16,512]{3,2,0,1:T(8,128)S(1)} async-done(((f32[2,8,16,512]{3,2,0,1:T(8,128)}), f32[2,8,16,512]{3,2,0,1:T(8,128)S(1)}, u32[]{:S(2)}, u32[]{:S(2)}) %all-to-all-start.1) | async-done | bytes 524320 | tf_op jit(solution)/shard_map/all_to_all | solution.py:92
  102.2 1.1 fusion.82
  103.4 1.1 fusion.2
  104.5 1.1 fusion.7
  107.3 1.6 fusion.6
  108.9 2.0 copy.66
  111.0 4.1 %all-to-all-start.9 = ((f32[2,1,128,512]{3,0,1,2:T(2,128)}), f32[2,1,128,512]{3,0,1,2:T(2,128)}, u32[]{:S(2)}, u32[]{:S(2)}) async-start(f32[2,1,128,512]{3,0,1,2:T(2,128)} %copy.66), calls=%async_computation.9 | async-start | bytes 1048576 | tf_op jit(solution)/shard_map/all_to_all | solution.py:103
  117.8 11.4 %all-to-all-done.9 = f32[2,1,128,512]{3,0,1,2:T(2,128)} async-done(((f32[2,1,128,512]{3,0,1,2:T(2,128)}), f32[2,1,128,512]{3,0,1,2:T(2,128)}, u32[]{:S(2)}, u32[]{:S(2)}) %all-to-all-start.9) | async-done | bytes 524320 | tf_op jit(solution)/shard_map/all_to_all | solution.py:103
  129.2 3.7 %all-to-all-start.10 = ((f32[2,1,128,512]{3,0,1,2:T(2,128)}), f32[2,1,128,512]{3,0,1,2:T(2,128)S(1)}, u32[]{:S(2)}, u32[]{:S(2)}) async-start(f32[2,1,128,512]{3,0,1,2:T(2,128)} %copy.69), calls=%async_computation.10 | async-start | bytes 1048576 | tf_op jit(solution)/shard_map/all_to_all | solution.py:104
  135.0 12.2 %all-to-all-done.10 = f32[2,1,128,512]{3,0,1,2:T(2,128)S(1)} async-done(((f32[2,1,128,512]{3,0,1,2:T(2,128)}), f32[2,1,128,512]{3,0,1,2:T(2,128)S(1)}, u32[]{:S(2)}, u32[]{:S(2)}) %all-to-all-start.10) | async-done | bytes 524320 | tf_op jit(solution)/shard_map/all_to_all | solution.py:104
  147.2 3.6 %all-to-all-start.4 = ((f32[1,1,128,512]{3,1,0,2:T(1,128)}), f32[1,1,128,512]{3,1,0,2:T(1,128)S(1)}, u32[]{:S(2)}, u32[]{:S(2)}) async-start(f32[1,1,128,512]{3,1,0,2:T(1,128)} %copy.56), calls=%async_computation.4 | async-start | bytes 524288 | tf_op jit(solution)/shard_map/all_to_all | solution.py:104
  152.9 1.1 copy.67
  154.1 5.7 %all-to-all-done.4 = f32[1,1,128,512]{3,1,0,2:T(1,128)S(1)} async-done(((f32[1,1,128,512]{3,1,0,2:T(1,128)}), f32[1,1,128,512]{3,1,0,2:T(1,128)S(1)}, u32[]{:S(2)}, u32[]{:S(2)}) %all-to-all-start.4) | async-done | bytes 262176 | tf_op jit(solution)/shard_map/all_to_all | solution.py:104
  159.8 3.6 %all-to-all-start.3 = ((f32[1,1,128,512]{3,1,0,2:T(1,128)}), f32[1,1,128,512]{3,1,0,2:T(1,128)S(1)}, u32[]{:S(2)}, u32[]{:S(2)}) async-start(f32[1,1,128,512]{3,1,0,2:T(1,128)} %copy.54), calls=%async_computation.3 | async-start | bytes 524288 | tf_op jit(solution)/shard_map/all_to_all | solution.py:103
  163.4 1.2 fusion.38
  164.6 1.2 fusion.4
  165.8 1.1 copy.74
  166.9 5.1 %all-to-all-done.3 = f32[1,1,128,512]{3,1,0,2:T(1,128)S(1)} async-done(((f32[1,1,128,512]{3,1,0,2:T(1,128)}), f32[1,1,128,512]{3,1,0,2:T(1,128)S(1)}, u32[]{:S(2)}, u32[]{:S(2)}) %all-to-all-start.3) | async-done | bytes 262176 | tf_op jit(solution)/shard_map/all_to_all | solution.py:103
  172.0 3.6 %all-to-all-start.11 = ((f32[2,8,16,512]{3,2,0,1:T(8,128)}), f32[2,8,16,512]{3,2,0,1:T(8,128)S(1)}, u32[]{:S(2)}, u32[]{:S(2)}) async-start(f32[2,8,16,512]{3,2,0,1:T(8,128)} %copy.74), calls=%async_computation.11 | async-start | bytes 1048576 | tf_op jit(solution)/shard_map/all_to_all | solution.py:110
  177.8 11.8 %all-to-all-done.11 = f32[2,8,16,512]{3,2,0,1:T(8,128)S(1)} async-done(((f32[2,8,16,512]{3,2,0,1:T(8,128)}), f32[2,8,16,512]{3,2,0,1:T(8,128)S(1)}, u32[]{:S(2)}, u32[]{:S(2)}) %all-to-all-start.11) | async-done | bytes 524320 | tf_op jit(solution)/shard_map/all_to_all | solution.py:110
  189.6 3.6 %all-to-all-start.5 = ((f32[1,8,16,512]{3,2,0,1:T(8,128)}), f32[1,8,16,512]{3,2,0,1:T(8,128)S(1)}, u32[]{:S(2)}, u32[]{:S(2)}) async-start(f32[1,8,16,512]{3,2,0,1:T(8,128)} %copy.60), calls=%async_computation.5 | async-start | bytes 524288 | tf_op jit(solution)/shard_map/all_to_all | solution.py:110
  193.3 8.6 %all-to-all-done.5 = f32[1,8,16,512]{3,2,0,1:T(8,128)S(1)} async-done(((f32[1,8,16,512]{3,2,0,1:T(8,128)}), f32[1,8,16,512]{3,2,0,1:T(8,128)S(1)}, u32[]{:S(2)}, u32[]{:S(2)}) %all-to-all-start.5) | async-done | bytes 262176 | tf_op jit(solution)/shard_map/all_to_all | solution.py:110
  201.9 1.7 fusion.52
  204.5 35.7 %all-reduce = (f32[3,7,512]{2,0,1:T(4,128)S(1)}, f32[512]{0:T(512)S(1)}) all-reduce(f32[3,7,512]{2,0,1:T(4,128)S(1)} %constant_dynamic-update-slice_fusion.2, f32[512]{0:T(512)S(1)} %get-tuple-element.38), channel_id=1, replica_groups=mesh['groups'=2,'seq'=8,'chan'=2] {'seq'}, use_global_device_ids=true, to_apply=%region_7.8 | all-reduce | flops 11264 | bytes 90112 | tf_op jit(solution)/shard_map/psum | solution.py:172
  240.4 2.0 collective-permute-start.3
  244.3 2.6 %collective-permute-done.3 = f32[3,3,512]{2,1,0:T(4,128)S(1)} collective-permute-done((f32[3,3,512]{2,1,0:T(4,128)S(1)}, f32[3,3,512]{2,1,0:T(4,128)S(1)}, u32[]{:S(2)}, u32[]{:S(2)}) %collective-permute-start.3) | collective-permute-done | bytes 18464 | tf_op jit(solution)/shard_map/ppermute | solution.py:17
  247.1 1.4 fusion.29
  (77 shorter events, 22.5 us)
Async XLA Ops:
  0.6 6.8 %copy-start.5 = (f32[3,7,512]{2,1,0:T(8,128)S(1)}, f32[3,7,512]{2,1,0:T(8,128)}, u32[]{:S(2)}) copy-start(f32[3,7,512]{2,1,0:T(8,128)} %param.7) | copy-start | bytes 129028
  1.4 7.4 %collective-permute-start.1 = (bf16[3,3,512]{2,1,0:T(4,128)(2,1)S(1)}, bf16[3,3,512]{2,1,0:T(4,128)(2,1)S(1)}, u32[]{:S(2)}, u32[]{:S(2)}) collective-permute-start(bf16[3,3,512]{2,1,0:T(4,128)(2,1)S(1)} %get-tuple-element.52), channel_id=1, source_target_pairs={{2,0},{4,2},{6,4},{8,6},{10,8},{12,10},{14,12},{0,14},{3,1},{5,3},... | collective-permute-start | bytes 27656 | tf_op jit(solution)/shard_map/ppermute | solution.py:20
  7.5 6.4 %collective-permute-start = (bf16[3,3,512]{2,1,0:T(4,128)(2,1)S(1)}, bf16[3,3,512]{2,1,0:T(4,128)(2,1)S(1)}, u32[]{:S(2)}, u32[]{:S(2)}) collective-permute-start(bf16[3,3,512]{2,1,0:T(4,128)(2,1)S(1)} %get-tuple-element.53), channel_id=1, source_target_pairs={{0,2},{2,4},{4,6},{6,8},{8,10},{10,12},{12,14},{14,0},{1,3},{3,5},... | collective-permute-start | bytes 27656 | tf_op jit(solution)/shard_map/ppermute | solution.py:17
  7.5 6.3 %copy-start = (bf16[3,128,512]{2,1,0:T(8,128)(2,1)S(1)}, bf16[3,128,512]{2,1,0:T(8,128)(2,1)}, u32[]{:S(2)}) copy-start(bf16[3,128,512]{2,1,0:T(8,128)(2,1)} %param.5) | copy-start | bytes 1179652
  13.8 0.9 copy-start.3
  15.8 11.6 %all-to-all-start.6 = ((f32[1,1,128,512]{3,1,0,2:T(1,128)}), f32[1,1,128,512]{3,1,0,2:T(1,128)S(1)}, u32[]{:S(2)}, u32[]{:S(2)}) async-start(f32[1,1,128,512]{3,1,0,2:T(1,128)} %copy.61), calls=%async_computation.6 | async-start | bytes 524288 | tf_op jit(solution)/shard_map/all_to_all | solution.py:88
  19.2 1.0 copy-start.4
  27.3 16.0 %all-to-all-start = ((f32[2,1,128,512]{3,0,1,2:T(2,128)}), f32[2,1,128,512]{3,0,1,2:T(2,128)S(1)}, u32[]{:S(2)}, u32[]{:S(2)}) async-start(f32[2,1,128,512]{3,0,1,2:T(2,128)} %copy.42), calls=%async_computation | async-start | bytes 1048576 | tf_op jit(solution)/shard_map/all_to_all | solution.py:88
  43.4 11.9 %all-to-all-start.7 = ((f32[1,8,16,512]{3,2,0,1:T(8,128)}), f32[1,8,16,512]{3,2,0,1:T(8,128)S(1)}, u32[]{:S(2)}, u32[]{:S(2)}) async-start(f32[1,8,16,512]{3,2,0,1:T(8,128)} %copy.64), calls=%async_computation.7 | async-start | bytes 524288 | tf_op jit(solution)/shard_map/all_to_all | solution.py:92
  55.3 11.6 %all-to-all-start.8 = ((f32[1,8,16,512]{3,2,0,1:T(8,128)}), f32[1,8,16,512]{3,2,0,1:T(8,128)S(1)}, u32[]{:S(2)}, u32[]{:S(2)}) async-start(f32[1,8,16,512]{3,2,0,1:T(8,128)} %copy.65), calls=%async_computation.8 | async-start | bytes 524288 | tf_op jit(solution)/shard_map/all_to_all | solution.py:93
  66.9 17.4 %all-to-all-start.2 = ((f32[2,8,16,512]{3,2,0,1:T(8,128)}), f32[2,8,16,512]{3,2,0,1:T(8,128)S(1)}, u32[]{:S(2)}, u32[]{:S(2)}) async-start(f32[2,8,16,512]{3,2,0,1:T(8,128)} %copy.49), calls=%async_computation.2 | async-start | bytes 1048576 | tf_op jit(solution)/shard_map/all_to_all | solution.py:93
  84.3 17.9 %all-to-all-start.1 = ((f32[2,8,16,512]{3,2,0,1:T(8,128)}), f32[2,8,16,512]{3,2,0,1:T(8,128)S(1)}, u32[]{:S(2)}, u32[]{:S(2)}) async-start(f32[2,8,16,512]{3,2,0,1:T(8,128)} %copy.46), calls=%async_computation.1 | async-start | bytes 1048576 | tf_op jit(solution)/shard_map/all_to_all | solution.py:92
  104.5 1.2 copy-start.1
  104.5 1.2 copy-start.2
  111.0 18.2 %all-to-all-start.9 = ((f32[2,1,128,512]{3,0,1,2:T(2,128)}), f32[2,1,128,512]{3,0,1,2:T(2,128)}, u32[]{:S(2)}, u32[]{:S(2)}) async-start(f32[2,1,128,512]{3,0,1,2:T(2,128)} %copy.66), calls=%async_computation.9 | async-start | bytes 1048576 | tf_op jit(solution)/shard_map/all_to_all | solution.py:103
  129.2 18.0 %all-to-all-start.10 = ((f32[2,1,128,512]{3,0,1,2:T(2,128)}), f32[2,1,128,512]{3,0,1,2:T(2,128)S(1)}, u32[]{:S(2)}, u32[]{:S(2)}) async-start(f32[2,1,128,512]{3,0,1,2:T(2,128)} %copy.69), calls=%async_computation.10 | async-start | bytes 1048576 | tf_op jit(solution)/shard_map/all_to_all | solution.py:104
  147.2 12.6 %all-to-all-start.4 = ((f32[1,1,128,512]{3,1,0,2:T(1,128)}), f32[1,1,128,512]{3,1,0,2:T(1,128)S(1)}, u32[]{:S(2)}, u32[]{:S(2)}) async-start(f32[1,1,128,512]{3,1,0,2:T(1,128)} %copy.56), calls=%async_computation.4 | async-start | bytes 524288 | tf_op jit(solution)/shard_map/all_to_all | solution.py:104
  159.8 12.2 %all-to-all-start.3 = ((f32[1,1,128,512]{3,1,0,2:T(1,128)}), f32[1,1,128,512]{3,1,0,2:T(1,128)S(1)}, u32[]{:S(2)}, u32[]{:S(2)}) async-start(f32[1,1,128,512]{3,1,0,2:T(1,128)} %copy.54), calls=%async_computation.3 | async-start | bytes 524288 | tf_op jit(solution)/shard_map/all_to_all | solution.py:103
  172.0 17.6 %all-to-all-start.11 = ((f32[2,8,16,512]{3,2,0,1:T(8,128)}), f32[2,8,16,512]{3,2,0,1:T(8,128)S(1)}, u32[]{:S(2)}, u32[]{:S(2)}) async-start(f32[2,8,16,512]{3,2,0,1:T(8,128)} %copy.74), calls=%async_computation.11 | async-start | bytes 1048576 | tf_op jit(solution)/shard_map/all_to_all | solution.py:110
  189.6 12.3 %all-to-all-start.5 = ((f32[1,8,16,512]{3,2,0,1:T(8,128)}), f32[1,8,16,512]{3,2,0,1:T(8,128)S(1)}, u32[]{:S(2)}, u32[]{:S(2)}) async-start(f32[1,8,16,512]{3,2,0,1:T(8,128)} %copy.60), calls=%async_computation.5 | async-start | bytes 524288 | tf_op jit(solution)/shard_map/all_to_all | solution.py:110
  193.2 8.7 %copy-start.6 = (f32[512]{0:T(512)S(1)}, f32[512]{0:T(512)}, u32[]{:S(2)}) copy-start(f32[512]{0:T(512)} %param.8) | copy-start | bytes 6148
  240.3 4.0 %collective-permute-start.2 = (f32[3,3,512]{2,1,0:T(4,128)S(1)}, f32[3,3,512]{2,1,0:T(4,128)S(1)}, u32[]{:S(2)}, u32[]{:S(2)}) collective-permute-start(f32[3,3,512]{2,1,0:T(4,128)S(1)} %get-tuple-element.46), channel_id=1, source_target_pairs={{2,0},{4,2},{6,4},{8,6},{10,8},{12,10},{14,12},{0,14},{3,1},{5,3},... | collective-permute-start | bytes 55304 | tf_op jit(solution)/shard_map/ppermute | solution.py:20
  240.4 6.6 %collective-permute-start.3 = (f32[3,3,512]{2,1,0:T(4,128)S(1)}, f32[3,3,512]{2,1,0:T(4,128)S(1)}, u32[]{:S(2)}, u32[]{:S(2)}) collective-permute-start(f32[3,3,512]{2,1,0:T(4,128)S(1)} %get-tuple-element.47), channel_id=1, source_target_pairs={{0,2},{2,4},{4,6},{6,8},{8,10},{10,12},{12,14},{14,0},{1,3},{3,5},... | collective-permute-start | bytes 55304 | tf_op jit(solution)/shard_map/ppermute | solution.py:17
where the time goes:
time: 250 us; the launch traced here: 248 us
  waiting for transfers between devices  114 us (46%)
  starting transfers between devices  51.5 us (21%)
  blocking collectives  35.7 us (14%)
  matrix products  21.8 us (9%)
  local copies, waits for them, and re-layouts  18.2 us (7%)
  other arithmetic  6.43 us (3%)
    psum x1, blocking collectives, body(): kernel_total, skip_total = lax.psum((kernel_part, skip_part), 'seq')  35.7 us
    dot_general x24, matrix products, apply_along(): jnp.einsum('k' + letters[axis_dim] + ',' + letters + '->' + target, matri...  21.8 us
    all_to_all x2, waiting for transfers between devices, sequence_inverse(): lax.all_to_all(pieces, 'seq', split_axis=1, concat_axis=2, tiled=True)  20.5 us
    all_to_all x2, waiting for transfers between devices, sequence_forward(): lax.all_to_all(imaginary, 'seq', split_axis=1, concat_axis=2, tiled=True)  18 us
    all_to_all x2, waiting for transfers between devices, sequence_inverse(): lax.all_to_all(imaginary, 'seq', split_axis=2, concat_axis=1, tiled=True)  17.8 us
    all_to_all x2, waiting for transfers between devices, sequence_forward(): lax.all_to_all(real_part, 'seq', split_axis=1, concat_axis=2, tiled=True)  16.7 us
    all_to_all x2, waiting for transfers between devices, sequence_inverse(): lax.all_to_all(real_part, 'seq', split_axis=2, concat_axis=1, tiled=True)  16.5 us
    all_to_all x2, waiting for transfers between devices, sequence_forward(): lax.all_to_all(signals[:, None], 'seq', split_axis=2, concat_axis=1, tile...  16.4 us
  transfers between devices with their start and end apart: 16, of which 15 were waited for; matrix products, arithmetic and copies ran while one was open for 12% of the time, Pallas kernels for 0%

commit v1 on v0

--- a/solution.py
+++ b/solution.py
@@ -1,11 +1,461 @@
+import functools
 import math
 
 import jax
 import jax.numpy as jnp
+import numpy as np
 from jax import lax
+from jax.experimental import pallas as pl
+from jax.experimental.pallas import tpu as pltpu
 from jax.sharding import PartitionSpec as P
 
 HIGHEST = lax.Precision.HIGHEST
+LANES = 128
+HALF = LANES // 2
+RIM = 8
+
+
+def turned(value, step, extent):
+    real_part, imaginary = value
+    step = step % extent
+    if step == 0:
+        return value
+    if 2 * step == extent:
+        return (-real_part, None if imaginary is None else -imaginary)
+    if 4 * step == extent:
+        return (None if imaginary is None else -imaginary, real_part)
+    if 4 * step == 3 * extent:
+        return (imaginary, -real_part)
+    cosine = math.cos(2.0 * math.pi * step / extent)
+    sine = math.sin(2.0 * math.pi * step / extent)
+    if imaginary is None:
+        return (real_part * cosine, real_part * sine)
+    return (real_part * cosine - imaginary * sine, imaginary * cosine + real_part * sine)
+
+
+def part_sum(left, right, sign):
+    if right is None:
+        return left
+    if left is None:
+        return right if sign > 0 else -right
+    return left + right if sign > 0 else left - right
+
+
+def real_spectrum(values):
+    extent = len(values)
+    if extent == 2:
+        return [(values[0] + values[1], None), (values[0] - values[1], None)]
+    even, odd = real_spectrum(values[0::2]), real_spectrum(values[1::2])
+    half = extent // 2
+
+    def entry(spectrum, index):
+        index = index % half
+        if 2 * index <= half:
+            return spectrum[index]
+        real_part, imaginary = spectrum[half - index]
+        return (real_part, None if imaginary is None else -imaginary)
+
+    found = []
+    for index in range(half + 1):
+        left, right = entry(even, index), turned(entry(odd, index), -index, extent)
+        found.append((part_sum(left[0], right[0], 1), part_sum(left[1], right[1], 1)))
+    return found
+
+
+def real_values(spectrum):
+    extent = 2 * (len(spectrum) - 1)
+    if extent == 2:
+        first, last = spectrum[0][0], spectrum[1][0]
+        return [first + last, first - last]
+    half = extent // 2
+    even, odd = [], []
+    for index in range(half // 2 + 1):
+        real_part, imaginary = spectrum[index]
+        if 2 * index == half:
+            even.append((2.0 * real_part, None))
+            odd.append((-2.0 * imaginary, None))
+            continue
+        other_real, other_imag = spectrum[half - index]
+        even.append(
+            (real_part + other_real, part_sum(imaginary, other_imag, -1))
+        )
+        odd.append(
+            turned(
+                (real_part - other_real, part_sum(imaginary, other_imag, 1)), index, extent
+            )
+        )
+    found = [None] * extent
+    found[0::2] = real_values(even)
+    found[1::2] = real_values(odd)
+    return found
+
+
+def fine_tables(slabs, width):
+    extent = slabs * width
+    coarse = np.arange(slabs // 2 + 1)[:, None, None]
+    fine = np.arange(width)[None, :, None]
+    place = np.arange(width)[None, None, :]
+    angles = ((coarse + slabs * fine) * place % extent) * (2.0 * np.pi / extent)
+    cosine, sine = np.cos(angles), np.sin(angles)
+    table = np.concatenate(
+        [np.concatenate([cosine, sine], 2), np.concatenate([-sine, cosine], 2)], 1
+    )
+    inverse = np.swapaxes(table, 1, 2) / (extent * math.sqrt(extent))
+    return table.astype(np.float32), inverse.astype(np.float32)
+
+
+def layer_kernel(
+    devices,
+    projected_ref,
+    filter_ref,
+    taps_ref,
+    gain_ref,
+    cotangent_ref,
+    forward_ref,
+    inverse_ref,
+    output_ref,
+    streams_ref,
+    filter_grad_ref,
+    taps_grad_ref,
+    gain_grad_ref,
+    send_pairs,
+    recv_pairs,
+    send_filter,
+    recv_filter,
+    send_grads,
+    recv_grads,
+    send_response,
+    recv_response,
+    send_sums,
+    recv_sums,
+    first_rim,
+    second_rim,
+    first_short,
+    second_short,
+    signal,
+    spectra,
+    send_sem,
+    recv_sem,
+):
+    rows = projected_ref.shape[1]
+    span = taps_ref.shape[1]
+    margin = span // 2
+    width = rows // 2
+    slabs = 2 * devices
+    extent = rows * devices
+    factor = 1.0 / math.sqrt(extent)
+    tiles = devices // 2
+    me = lax.axis_index("seq")
+    odd = lax.rem(me, 2) == 1
+
+    def low_lanes(shape):
+        return lax.broadcasted_iota(jnp.int32, shape, 1) < HALF
+
+    def swap(value):
+        return pltpu.roll(value, HALF, 1)
+
+    def join(first, second, parity):
+        low = low_lanes(first.shape)
+        if parity == 0:
+            return jnp.where(low, first, swap(second))
+        return jnp.where(low, swap(first), second)
+
+    def wide(value):
+        return value.astype(jnp.float32)
+
+    def copy_to(kind, hop, source, target, slot, peer):
+        return pltpu.make_async_remote_copy(
+            src_ref=source,
+            dst_ref=target.at[slot],
+            send_sem=send_sem.at[kind, hop],
+            recv_sem=recv_sem.at[kind, hop],
+            device_id={"seq": peer},
+            device_id_type=pl.DeviceIdType.MESH,
+        )
+
+    def peer_at(hop):
+        return lax.rem(me + hop, devices)
+
+    def source_at(hop):
+        return lax.rem(me + devices - hop, devices)
+
+    barrier = pltpu.get_barrier_semaphore()
+    for hop in range(1, devices):
+        pl.semaphore_signal(
+            barrier, inc=1, device_id={"seq": peer_at(hop)}, device_id_type=pl.DeviceIdType.MESH
+        )
+
+    for tile in range(tiles):
+        lanes = slice(tile * LANES, (tile + 1) * LANES)
+        gate, left, right = [wide(projected_ref[s, :, lanes]) for s in range(3)]
+        upstream = wide(cotangent_ref[:, lanes])
+        for parity in range(2):
+            send_pairs[2 * tile + parity, 0] = join(left, gate, parity).astype(jnp.bfloat16)
+            send_pairs[2 * tile + parity, 1] = join(right, upstream, parity).astype(jnp.bfloat16)
+    pl.semaphore_wait(barrier, devices - 1)
+    for hop in range(1, devices):
+        peer = peer_at(hop)
+        copy_to(0, hop, send_pairs.at[peer], recv_pairs, me, peer).start()
+    for tile in range(tiles):
+        lanes = slice(tile * LANES, (tile + 1) * LANES)
+        whole = filter_ref[:, lanes]
+        coarse = wide(whole.astype(jnp.bfloat16))
+        for parity in range(2):
+            send_filter[2 * tile + parity] = join(coarse, whole - coarse, parity).astype(
+                jnp.bfloat16
+            )
+    for hop in range(1, devices):
+        peer = peer_at(hop)
+        copy_to(1, hop, send_filter.at[peer], recv_filter, me, peer).start()
+    recv_pairs[me] = send_pairs[me]
+    recv_filter[me] = send_filter[me]
+
+    own = pl.ds(pl.multiple_of((me // 2) * LANES, LANES), LANES)
+
+    def own_pair(first, second):
+        return jnp.where(odd, join(first, second, 1), join(first, second, 0))
+
+    gate_taps, left_taps, right_taps = [taps_ref[s, :, own] for s in range(3)]
+    first_taps = own_pair(left_taps, gate_taps)
+    centre = wide(lax.broadcasted_iota(jnp.int32, (span, LANES), 0) == margin)
+    second_taps = jnp.where(
+        low_lanes((span, LANES)), own_pair(right_taps, right_taps), centre
+    )
+    own_gain = gain_ref[:, own]
+    gain = own_pair(own_gain, own_gain)
+
+    def wait_from(kind, source, target):
+        for hop in range(1, devices):
+            copy_to(kind, hop, source.at[peer_at(hop)], target, source_at(hop), peer_at(hop)).wait()
+
+    def close_rim(rim):
+        rim[0:RIM] = rim[extent : extent + RIM]
+        rim[extent + RIM : extent + 2 * RIM] = rim[RIM : 2 * RIM]
+
+    wait_from(0, send_pairs, recv_pairs)
+    for block in range(devices):
+        here = slice(RIM + block * rows, RIM + (block + 1) * rows)
+        first_rim[0, here] = wide(recv_pairs[block, 0])
+        second_rim[0, here] = wide(recv_pairs[block, 1])
+    close_rim(first_rim.at[0])
+    close_rim(second_rim.at[0])
+
+    def shorten(slab, total):
+        start = pl.multiple_of(slab * width, width)
+        around_first = first_rim[0, pl.ds(start, width + 2 * RIM)]
+        around_second = second_rim[0, pl.ds(start, width + 2 * RIM)]
+        first = jnp.zeros((width, LANES), jnp.float32)
+        second = jnp.zeros((width, LANES), jnp.float32)
+        for tap in range(span):
+            low = RIM + tap - margin
+            first = first + first_taps[tap : tap + 1] * around_first[low : low + width]
+            second = second + second_taps[tap : tap + 1] * around_second[low : low + width]
+        product = first * second
+        first_short[pl.ds(start, width)] = first
+        second_short[pl.ds(start, width)] = second
+        signal[pl.ds(start, width)] = product
+        return total + jnp.sum((product * swap(product)).reshape(-1, 8, LANES), axis=0)
+
+    gain_sum = lax.fori_loop(0, slabs, shorten, jnp.zeros((8, LANES), jnp.float32))
+
+    def put_spectrum(found, start, count, lanes):
+        for index, (real_part, imaginary) in enumerate(found):
+            if imaginary is None:
+                imaginary = jnp.zeros_like(real_part)
+            spectra[index, pl.ds(start, count), lanes] = real_part
+            spectra[index, pl.ds(width + start, count), lanes] = imaginary
+
+    def signal_spectrum(step, carry):
+        start = pl.multiple_of(step * 8, 8)
+        values = [signal[pl.ds(slab * width + start, 8)] for slab in range(slabs)]
+        put_spectrum(real_spectrum(values), start, 8, slice(0, LANES))
+        return carry
+
+    lax.fori_loop(0, width // 8, signal_spectrum, 0)
+
+    wait_from(1, send_filter, recv_filter)
+
+    def filter_spectrum(step, carry):
+        start = pl.multiple_of(step * 16, 16)
+        values = []
+        for slab in range(slabs):
+            packed = wide(recv_filter[slab // 2, pl.ds((slab % 2) * width + start, 16)])
+            values.append(packed + swap(packed))
+        put_spectrum(real_spectrum(values), start, 16, slice(LANES, 2 * LANES))
+        return carry
+
+    lax.fori_loop(0, width // 16, filter_spectrum, 0)
+
+    sign = jnp.where(low_lanes((width, LANES)), 1.0, -1.0).astype(jnp.float32)
+    for index in range(slabs // 2 + 1):
+        found = jnp.dot(forward_ref[index], spectra[index], precision=HIGHEST)
+        real_part, imaginary = found[:width, :LANES], found[width:, :LANES]
+        filter_real, filter_imag = found[:width, LANES:], sign * found[width:, LANES:]
+        other_real, other_imag = swap(real_part), swap(imaginary)
+        spectra[index, 0:width, 0:LANES] = filter_real * real_part - filter_imag * imaginary
+        spectra[index, width:, 0:LANES] = filter_real * imaginary + filter_imag * real_part
+        spectra[index, 0:width, LANES:] = real_part * other_real + imaginary * other_imag
+        spectra[index, width:, LANES:] = sign * (real_part * other_imag - imaginary * other_real)
+        spectra[index] = jnp.dot(inverse_ref[index], spectra[index], precision=HIGHEST)
+
+    def get_spectrum(start, count, lanes):
+        found = []
+        for index in range(slabs // 2 + 1):
+            real_part = spectra[index, pl.ds(start, count), lanes]
+            imaginary = None
+            if 0 < index < slabs // 2:
+                imaginary = spectra[index, pl.ds(width + start, count), lanes]
+            found.append((real_part, imaginary))
+        return found
+
+    def filter_back(step, carry):
+        start = pl.multiple_of(step * 16, 16)
+        values = real_values(get_spectrum(start, 16, slice(LANES, 2 * LANES)))
+        low = low_lanes((16, LANES))
+        for slab, value in enumerate(values):
+            coarse = wide(value.astype(jnp.bfloat16))
+            send_response[slab // 2, pl.ds((slab % 2) * width + start, 16)] = jnp.where(
+                low, coarse, value - coarse
+            ).astype(jnp.bfloat16)
+        return carry
+
+    lax.fori_loop(0, width // 16, filter_back, 0)
+    for hop in range(1, devices):
+        peer = peer_at(hop)
+        copy_to(2, hop, send_response.at[peer], recv_response, me, peer).start()
+    recv_response[me] = send_response[me]
+
+    def signal_back(step, carry):
+        start = pl.multiple_of(step * 8, 8)
+        values = real_values(get_spectrum(start, 8, slice(0, LANES)))
+        for slab, value in enumerate(values):
+            place = pl.ds(slab * width + start, 8)
+            back = swap(value + gain * signal[place])
+            inner = pl.ds(RIM + slab * width + start, 8)
+            first_rim[1, inner] = back * second_short[place]
+            second_rim[1, inner] = back * first_short[place]
+        return carry
+
+    lax.fori_loop(0, width // 8, signal_back, 0)
+    close_rim(first_rim.at[1])
+    close_rim(second_rim.at[1])
+
+    def grads(block, sums):
+        sums = list(sums)
+        for part in range(2):
+            start = pl.multiple_of(block * rows + part * width, width)
+            inner = pl.ds(start, width + 2 * RIM)
+            for which, (rim, taps) in enumerate(((first_rim, first_taps), (second_rim, second_taps))):
+                around = rim[1, inner]
+                streams = rim[0, inner]
+                here = around[RIM : RIM + width]
+                total = jnp.zeros((width, LANES), jnp.float32)
+                for tap in range(span):
+                    low = RIM + margin - tap
+                    total = total + taps[tap : tap + 1] * around[low : low + width]
+                    low = RIM + tap - margin
+                    sums[which * span + tap] = sums[which * span + tap] + jnp.sum(
+                        (here * streams[low : low + width]).reshape(-1, 8, LANES), axis=0
+                    )
+                send_grads[block, which, part * width : (part + 1) * width] = total.astype(
+                    jnp.bfloat16
+                )
+        return tuple(sums)
+
+    def step_grads(hop, sums):
+        peer = peer_at(hop)
+        sums = grads(peer, sums)
+        copy_to(3, hop, send_grads.at[peer], recv_grads, me, peer).start()
+        return sums
+
+    sums = tuple(jnp.zeros((8, LANES), jnp.float32) for _ in range(2 * span))
+    sums = lax.fori_loop(1, devices, step_grads, sums)
+    sums = grads(me, sums)
+    for index, value in enumerate(sums + (gain_sum,)):
+        send_sums[index : index + 1] = factor * jnp.sum(value, axis=0, keepdims=True)
+    for hop in range(1, devices):
+        copy_to(4, hop, send_sums, recv_sums, me, peer_at(hop)).start()
+    recv_sums[me] = send_sums[...]
+    recv_grads[me] = send_grads[me]
+
+    def split(first, second):
+        low = low_lanes(first.shape)
+        return jnp.where(low, first, swap(second)), jnp.where(low, swap(first), second)
+
+    wait_from(2, send_response, recv_response)
+    for tile in range(tiles):
+        lanes = slice(tile * LANES, (tile + 1) * LANES)
+        first, second = wide(recv_response[2 * tile]), wide(recv_response[2 * tile + 1])
+        filter_grad_ref[:, lanes] = jnp.where(
+            low_lanes(first.shape), first + swap(first), second + swap(second)
+        )
+    wait_from(3, send_grads, recv_grads)
+    for tile in range(tiles):
+        lanes = slice(tile * LANES, (tile + 1) * LANES)
+        for which, targets in enumerate(
+            ((streams_ref.at[1], streams_ref.at[0]), (streams_ref.at[2], output_ref))
+        ):
+            pieces = split(wide(recv_grads[2 * tile, which]), wide(recv_grads[2 * tile + 1, which]))
+            for target, piece in zip(targets, pieces):
+                target[:, lanes] = piece.astype(jnp.bfloat16)
+    for hop in range(1, devices):
+        copy_to(4, hop, send_sums, recv_sums, source_at(hop), peer_at(hop)).wait()
+    for tile in range(tiles):
+        lanes = slice(tile * LANES, (tile + 1) * LANES)
+        low_part, high_part = split(recv_sums[2 * tile], recv_sums[2 * tile + 1])
+        taps_grad_ref[1, :, lanes] = low_part[0:span]
+        taps_grad_ref[0, :, lanes] = high_part[0:span]
+        taps_grad_ref[2, :, lanes] = low_part[span : 2 * span]
+        gain_grad_ref[:, lanes] = low_part[2 * span : 2 * span + 1]
+
+
+def packed_body(devices, projected, long_filter, short_kernel, skip_gain, cotangent):
+    rows, channels = long_filter.shape
+    span = short_kernel.shape[1]
+    extent = rows * devices
+    slabs = 2 * devices
+    tables = fine_tables(slabs, rows // 2)
+    sums_rows = -(-(2 * span + 1) // 8) * 8
+    block = (devices, rows, LANES)
+    pair = (devices, 2, rows, LANES)
+    narrow, full = jnp.bfloat16, jnp.float32
+    in_vmem = pl.BlockSpec(memory_space=pltpu.VMEM)
+    found = pl.pallas_call(
+        functools.partial(layer_kernel, devices),
+        out_shape=(
+            jax.ShapeDtypeStruct((rows, channels), narrow),
+            jax.ShapeDtypeStruct((3, rows, channels), narrow),
+            jax.ShapeDtypeStruct((rows, channels), full),
+            jax.ShapeDtypeStruct(short_kernel.shape, full),
+            jax.ShapeDtypeStruct((1, channels), full),
+        ),
+        in_specs=[in_vmem] * 7,
+        out_specs=(in_vmem,) * 5,
+        scratch_shapes=[
+            pltpu.VMEM(pair, narrow),
+            pltpu.VMEM(pair, narrow),
+            pltpu.VMEM(block, narrow),
+            pltpu.VMEM(block, narrow),
+            pltpu.VMEM(pair, narrow),
+            pltpu.VMEM(pair, narrow),
+            pltpu.VMEM(block, narrow),
+            pltpu.VMEM(block, narrow),
+            pltpu.VMEM((sums_rows, LANES), full),
+            pltpu.VMEM((devices, sums_rows, LANES), full),
+            pltpu.VMEM((2, extent + 2 * RIM, LANES), full),
+            pltpu.VMEM((2, extent + 2 * RIM, LANES), full),
+            pltpu.VMEM((extent, LANES), full),
+            pltpu.VMEM((extent, LANES), full),
+            pltpu.VMEM((extent, LANES), full),
+            pltpu.VMEM((slabs // 2 + 1, rows, 2 * LANES), full),
+            pltpu.SemaphoreType.DMA((5, devices)),
+            pltpu.SemaphoreType.DMA((5, devices)),
+        ],
+        compiler_params=pltpu.CompilerParams(
+            collective_id=0, has_side_effects=True, vmem_limit_bytes=40 * 1024 * 1024
+        ),
+    )(projected, long_filter, short_kernel, skip_gain[None], cotangent, *tables)
+    return (*found[:4], found[4][0])
 
 
 def with_halo(block, sides, width):
@@ -187,8 +637,16 @@
         P("chan"),
         P(("groups", "seq"), "chan"),
     )
+    devices = mesh.shape["seq"]
+
+    def run(projected, *others):
+        rows, channels = projected.shape[1:]
+        if channels == HALF * devices and rows == LANES and devices & (devices - 1) == 0:
+            return packed_body(devices, projected, *others)
+        return body(projected, *others)
+
     return jax.shard_map(
-        body,
+        run,
         mesh=mesh,
         in_specs=placed,
         out_specs=(

time: 250 us -> 57.4 us (0.23)
  waiting for transfers between devices: 114 us -> 0 us
  starting transfers between devices: 51.5 us -> 0 us
  Pallas kernels: 0 us -> 46.6 us
  blocking collectives: 35.7 us -> 0 us
  matrix products: 21.8 us -> 0 us
  local copies, waits for them, and re-layouts: 18.2 us -> 9.75 us
  other arithmetic: 6.43 us -> 0 us
    all_to_all x12 -> x0, waiting for transfers between devices: 106 us -> none  [the longest x2 20.5 us: sequence_inverse(): lax.all_to_all(pieces, 'seq', split_axis=1, concat_axis=2, tiled=True)]
    pallas_call x0 -> x1, Pallas kernels: none -> 46.6 us  [packed_body(): pl.pallas_call(functools.partial(layer_kernel, devices), out_shape=(jax.S...]
    all_to_all x12 -> x0, starting transfers between devices: 43.4 us -> none  [the longest x2 7.73 us: sequence_inverse(): lax.all_to_all(real_part, 'seq', split_axis=2, concat_axis=1, tiled=True)]
    psum x1 -> x0, blocking collectives: 35.7 us -> none  [body(): kernel_total, skip_total = lax.psum((kernel_part, skip_part), 'seq')]
    dot_general x24 -> x0, matrix products: 21.8 us -> none  [apply_along(): jnp.einsum('k' + letters[axis_dim] + ',' + letters + '->' + target, matri...]
    ppermute x4 -> x0, starting transfers between devices: 8.1 us -> none  [the longest x2 6.09 us: with_halo(): lax.ppermute(lax.slice_in_dim(block, 0, width, axis=dim), axis, backward)]
    ppermute x4 -> x0, waiting for transfers between devices: 7.8 us -> none  [the longest x2 7.59 us: with_halo(): lax.ppermute(lax.slice_in_dim(block, block.shape[dim] - width, None, axis...]
    unnamed x29 -> x19, local copies, waits for them, and re-layouts: 2.98 us -> 9.75 us
  transfers between devices with their start and end apart: 16 -> 0, of which waited for: 15 -> 0; matrix products, arithmetic and copies ran while one was open for 12% -> 0% of each run, Pallas kernels for 0% -> 0%
where the time goes in v1:
time: 57.4 us; the launch traced here: 57 us
  Pallas kernels  46.6 us (81%)
  local copies, waits for them, and re-layouts  9.75 us (17%)
  between operations  0.66 us (1%)
    pallas_call x1, Pallas kernels, packed_body(): pl.pallas_call(functools.partial(layer_kernel, devices), out_shape=(jax.S...  46.6 us
    unnamed x19, local copies, waits for them, and re-layouts  9.75 us

profile of v1, /device:TPU:0, one launch (start us, length us, event | category | flops | bytes accessed | tf_op | source)
XLA Modules:
  0.0 57.0 jit_solution(2940678495329463778)
XLA Ops:
  0.6 0.0 copy-start
  0.6 1.1 %copy-done = f32[9,128,128]{2,1,0:T(8,128)S(1)} copy-done((f32[9,128,128]{2,1,0:T(8,128)S(1)}, f32[9,128,128]{2,1,0:T(8,128)}, u32[]{:S(2)}) %copy-start) | copy-done | bytes 589848
  1.7 0.0 copy-start.1
  1.7 1.1 %copy-done.1 = f32[9,128,128]{2,1,0:T(8,128)S(1)} copy-done((f32[9,128,128]{2,1,0:T(8,128)S(1)}, f32[9,128,128]{2,1,0:T(8,128)}, u32[]{:S(2)}) %copy-start.1) | copy-done | bytes 589848
  2.8 0.0 copy-start.2
  2.8 1.0 %copy-done.2 = bf16[3,128,512]{2,1,0:T(8,128)(2,1)S(1)} copy-done((bf16[3,128,512]{2,1,0:T(8,128)(2,1)S(1)}, bf16[3,128,512]{2,1,0:T(8,128)(2,1)}, u32[]{:S(2)}) %copy-start.2) | copy-done | bytes 393240
  3.8 0.0 copy-start.3
  3.8 0.9 %copy-done.3 = f32[128,512]{1,0:T(8,128)S(1)} copy-done((f32[128,512]{1,0:T(8,128)S(1)}, f32[128,512]{1,0:T(8,128)}, u32[]{:S(2)}) %copy-start.3) | copy-done | bytes 262168
  4.7 0.0 copy-start.4
  4.7 0.9 %copy-done.4 = bf16[128,512]{1,0:T(8,128)(2,1)S(1)} copy-done((bf16[128,512]{1,0:T(8,128)(2,1)S(1)}, bf16[128,512]{1,0:T(8,128)(2,1)}, u32[]{:S(2)}) %copy-start.4) | copy-done | bytes 131096
  5.6 0.0 copy-start.5
  5.6 0.8 %copy-done.5 = f32[3,7,512]{2,1,0:T(8,128)S(1)} copy-done((f32[3,7,512]{2,1,0:T(8,128)S(1)}, f32[3,7,512]{2,1,0:T(8,128)}, u32[]{:S(2)}) %copy-start.5) | copy-done | bytes 43032
  6.4 0.0 copy-start.6
  6.4 0.7 %copy-done.6 = f32[512]{0:T(512)S(1)} copy-done((f32[512]{0:T(512)S(1)}, f32[512]{0:T(512)}, u32[]{:S(2)}) %copy-start.6) | copy-done | bytes 2072
  7.1 46.6 %shard_map.110 = (bf16[128,512]{1,0:T(8,128)(2,1)S(1)}, bf16[3,128,512]{2,1,0:T(8,128)(2,1)S(1)}, f32[128,512]{1,0:T(8,128)S(1)}, f32[3,7,512]{2,1,0:T(8,128)S(1)}, f32[1,512]{1,0:T(1,128)S(1)}) custom-call(bf16[3,128,512]{2,1,0:T(8,128)(2,1)S(1)} %copy-done.2, f32[128,512]{1,0:T(8,128)S(1)} %copy-done.3, f32[3,7,512]{2,1,0:T(8,128)S(1)} %copy-done.5, ...), custom_call_target="tpu_custom_call" | custom-call | tf_op jit(solution)/shard_map/pallas_call | solution.py:423
  53.7 0.7 %copy.17 = bf16[128,512]{1,0:T(8,128)(2,1)} copy(bf16[128,512]{1,0:T(8,128)(2,1)S(1)} %get-tuple-element.20) | data formatting | bytes 262144
  54.3 0.7 %copy.18 = bf16[3,128,512]{2,1,0:T(8,128)(2,1)} copy(bf16[3,128,512]{2,1,0:T(8,128)(2,1)S(1)} %get-tuple-element.21) | data formatting | bytes 786432
  55.1 0.7 %copy.19 = f32[128,512]{1,0:T(8,128)} copy(f32[128,512]{1,0:T(8,128)S(1)} %get-tuple-element.22) | data formatting | bytes 524288
  55.8 0.6 %copy.20 = f32[3,7,512]{2,1,0:T(8,128)} copy(f32[3,7,512]{2,1,0:T(8,128)S(1)} %get-tuple-element.23) | data formatting | bytes 86016
  56.4 0.6 %copy.21 = f32[512]{0:T(512)} copy(f32[512]{0:T(512)S(1)} %bitcast.3) | data formatting | bytes 4096
Async XLA Ops:
  0.6 1.1 %copy-start = (f32[9,128,128]{2,1,0:T(8,128)S(1)}, f32[9,128,128]{2,1,0:T(8,128)}, u32[]{:S(2)}) copy-start(f32[9,128,128]{2,1,0:T(8,128)} %constant.5.clone.inverse_ref) | copy-start | bytes 1769476
  1.7 1.1 %copy-start.1 = (f32[9,128,128]{2,1,0:T(8,128)S(1)}, f32[9,128,128]{2,1,0:T(8,128)}, u32[]{:S(2)}) copy-start(f32[9,128,128]{2,1,0:T(8,128)} %constant.4.clone.forward_ref) | copy-start | bytes 1769476
  2.8 1.0 %copy-start.2 = (bf16[3,128,512]{2,1,0:T(8,128)(2,1)S(1)}, bf16[3,128,512]{2,1,0:T(8,128)(2,1)}, u32[]{:S(2)}) copy-start(bf16[3,128,512]{2,1,0:T(8,128)(2,1)} %projected_ref.1) | copy-start | bytes 1179652
  3.8 0.9 %copy-start.3 = (f32[128,512]{1,0:T(8,128)S(1)}, f32[128,512]{1,0:T(8,128)}, u32[]{:S(2)}) copy-start(f32[128,512]{1,0:T(8,128)} %filter_ref.1) | copy-start | bytes 786436
  4.7 0.9 %copy-start.4 = (bf16[128,512]{1,0:T(8,128)(2,1)S(1)}, bf16[128,512]{1,0:T(8,128)(2,1)}, u32[]{:S(2)}) copy-start(bf16[128,512]{1,0:T(8,128)(2,1)} %cotangent_ref.1) | copy-start | bytes 393220
  5.6 0.8 %copy-start.5 = (f32[3,7,512]{2,1,0:T(8,128)S(1)}, f32[3,7,512]{2,1,0:T(8,128)}, u32[]{:S(2)}) copy-start(f32[3,7,512]{2,1,0:T(8,128)} %taps_ref.1) | copy-start | bytes 129028
  6.4 0.7 %copy-start.6 = (f32[512]{0:T(512)S(1)}, f32[512]{0:T(512)}, u32[]{:S(2)}) copy-start(f32[512]{0:T(512)} %param.10) | copy-start | bytes 6148

commit v2 on v1

--- a/solution.py
+++ b/solution.py
@@ -13,6 +13,7 @@
 LANES = 128
 HALF = LANES // 2
 RIM = 8
+LIMIT = 64 * 1024 * 1024 - 1024 * 1024
 
 
 def turned(value, step, extent):
@@ -106,18 +107,25 @@
 
 def layer_kernel(
     devices,
-    projected_ref,
-    filter_ref,
-    taps_ref,
-    gain_ref,
-    cotangent_ref,
-    forward_ref,
-    inverse_ref,
+    projected_in,
+    cotangent_in,
+    filter_in,
+    taps_in,
+    gain_in,
+    forward_in,
+    inverse_in,
     output_ref,
     streams_ref,
     filter_grad_ref,
     taps_grad_ref,
     gain_grad_ref,
+    projected_ref,
+    cotangent_ref,
+    filter_ref,
+    taps_ref,
+    gain_ref,
+    forward_ref,
+    inverse_ref,
     send_pairs,
     recv_pairs,
     send_filter,
@@ -133,10 +141,29 @@
     first_short,
     second_short,
     signal,
-    spectra,
+    signal_spectra,
+    product_spectra,
+    filter_spectra,
+    load_sem,
     send_sem,
     recv_sem,
 ):
+    arguments = (projected_in, cotangent_in, filter_in, taps_in, gain_in, forward_in, inverse_in)
+    held = (
+        projected_ref,
+        cotangent_ref,
+        filter_ref,
+        taps_ref,
+        gain_ref,
+        forward_ref,
+        inverse_ref,
+    )
+    loads = [
+        pltpu.make_async_copy(source, target, load_sem.at[index])
+        for index, (source, target) in enumerate(zip(arguments, held))
+    ]
+    for load in loads:
+        load.start()
     rows = projected_ref.shape[1]
     span = taps_ref.shape[1]
     margin = span // 2
@@ -185,6 +212,8 @@
             barrier, inc=1, device_id={"seq": peer_at(hop)}, device_id_type=pl.DeviceIdType.MESH
         )
 
+    loads[0].wait()
+    loads[1].wait()
     for tile in range(tiles):
         lanes = slice(tile * LANES, (tile + 1) * LANES)
         gate, left, right = [wide(projected_ref[s, :, lanes]) for s in range(3)]
@@ -196,6 +225,7 @@
     for hop in range(1, devices):
         peer = peer_at(hop)
         copy_to(0, hop, send_pairs.at[peer], recv_pairs, me, peer).start()
+    loads[2].wait()
     for tile in range(tiles):
         lanes = slice(tile * LANES, (tile + 1) * LANES)
         whole = filter_ref[:, lanes]
@@ -210,6 +240,8 @@
     recv_pairs[me] = send_pairs[me]
     recv_filter[me] = send_filter[me]
 
+    for load in loads[3:5]:
+        load.wait()
     own = pl.ds(pl.multiple_of((me // 2) * LANES, LANES), LANES)
 
     def own_pair(first, second):
@@ -258,59 +290,50 @@
 
     gain_sum = lax.fori_loop(0, slabs, shorten, jnp.zeros((8, LANES), jnp.float32))
 
-    def put_spectrum(found, start, count, lanes):
+    def put_spectrum(spectra, found, start, count):
         for index, (real_part, imaginary) in enumerate(found):
             if imaginary is None:
                 imaginary = jnp.zeros_like(real_part)
-            spectra[index, pl.ds(start, count), lanes] = real_part
-            spectra[index, pl.ds(width + start, count), lanes] = imaginary
+            spectra[index, pl.ds(start, count)] = real_part
+            spectra[index, pl.ds(width + start, count)] = imaginary
 
     def signal_spectrum(step, carry):
         start = pl.multiple_of(step * 8, 8)
         values = [signal[pl.ds(slab * width + start, 8)] for slab in range(slabs)]
-        put_spectrum(real_spectrum(values), start, 8, slice(0, LANES))
+        put_spectrum(signal_spectra, real_spectrum(values), start, 8)
         return carry
 
     lax.fori_loop(0, width // 8, signal_spectrum, 0)
 
-    wait_from(1, send_filter, recv_filter)
-
-    def filter_spectrum(step, carry):
-        start = pl.multiple_of(step * 16, 16)
-        values = []
-        for slab in range(slabs):
-            packed = wide(recv_filter[slab // 2, pl.ds((slab % 2) * width + start, 16)])
-            values.append(packed + swap(packed))
-        put_spectrum(real_spectrum(values), start, 16, slice(LANES, 2 * LANES))
-        return carry
-
-    lax.fori_loop(0, width // 16, filter_spectrum, 0)
-
+    for load in loads[5:]:
+        load.wait()
     sign = jnp.where(low_lanes((width, LANES)), 1.0, -1.0).astype(jnp.float32)
     for index in range(slabs // 2 + 1):
-        found = jnp.dot(forward_ref[index], spectra[index], precision=HIGHEST)
-        real_part, imaginary = found[:width, :LANES], found[width:, :LANES]
-        filter_real, filter_imag = found[:width, LANES:], sign * found[width:, LANES:]
+        found = jnp.dot(forward_ref[index], signal_spectra[index], precision=HIGHEST)
+        signal_spectra[index] = found
+        real_part, imaginary = found[:width], found[width:]
         other_real, other_imag = swap(real_part), swap(imaginary)
-        spectra[index, 0:width, 0:LANES] = filter_real * real_part - filter_imag * imaginary
-        spectra[index, width:, 0:LANES] = filter_real * imaginary + filter_imag * real_part
-        spectra[index, 0:width, LANES:] = real_part * other_real + imaginary * other_imag
-        spectra[index, width:, LANES:] = sign * (real_part * other_imag - imaginary * other_real)
-        spectra[index] = jnp.dot(inverse_ref[index], spectra[index], precision=HIGHEST)
-
-    def get_spectrum(start, count, lanes):
+        product = jnp.concatenate(
+            [
+                real_part * other_real + imaginary * other_imag,
+                sign * (real_part * other_imag - imaginary * other_real),
+            ],
+            axis=0,
+        )
+        product_spectra[index] = jnp.dot(inverse_ref[index], product, precision=HIGHEST)
+
+    def get_spectrum(spectra, start, count):
         found = []
         for index in range(slabs // 2 + 1):
-            real_part = spectra[index, pl.ds(start, count), lanes]
             imaginary = None
             if 0 < index < slabs // 2:
-                imaginary = spectra[index, pl.ds(width + start, count), lanes]
-            found.append((real_part, imaginary))
+                imaginary = spectra[index, pl.ds(width + start, count)]
+            found.append((spectra[index, pl.ds(start, count)], imaginary))
         return found
 
     def filter_back(step, carry):
         start = pl.multiple_of(step * 16, 16)
-        values = real_values(get_spectrum(start, 16, slice(LANES, 2 * LANES)))
+        values = real_values(get_spectrum(product_spectra, start, 16))
         low = low_lanes((16, LANES))
         for slab, value in enumerate(values):
             coarse = wide(value.astype(jnp.bfloat16))
@@ -325,9 +348,35 @@
         copy_to(2, hop, send_response.at[peer], recv_response, me, peer).start()
     recv_response[me] = send_response[me]
 
+    wait_from(1, send_filter, recv_filter)
+
+    def filter_spectrum(step, carry):
+        start = pl.multiple_of(step * 16, 16)
+        values = []
+        for slab in range(slabs):
+            packed = wide(recv_filter[slab // 2, pl.ds((slab % 2) * width + start, 16)])
+            values.append(packed + swap(packed))
+        put_spectrum(filter_spectra, real_spectrum(values), start, 16)
+        return carry
+
+    lax.fori_loop(0, width // 16, filter_spectrum, 0)
+
+    for index in range(slabs // 2 + 1):
+        found = jnp.dot(forward_ref[index], filter_spectra[index], precision=HIGHEST)
+        filter_real, filter_imag = found[:width], sign * found[width:]
+        real_part, imaginary = signal_spectra[index, :width], signal_spectra[index, width:]
+        product = jnp.concatenate(
+            [
+                filter_real * real_part - filter_imag * imaginary,
+                filter_real * imaginary + filter_imag * real_part,
+            ],
+            axis=0,
+        )
+        filter_spectra[index] = jnp.dot(inverse_ref[index], product, precision=HIGHEST)
+
     def signal_back(step, carry):
         start = pl.multiple_of(step * 8, 8)
-        values = real_values(get_spectrum(start, 8, slice(0, LANES)))
+        values = real_values(get_spectrum(filter_spectra, start, 8))
         for slab, value in enumerate(values):
             place = pl.ds(slab * width + start, 8)
             back = swap(value + gain * signal[place])
@@ -409,6 +458,15 @@
         gain_grad_ref[:, lanes] = low_part[2 * span : 2 * span + 1]
 
 
+def store_kernel(*refs):
+    sem = refs[10]
+    copies = [pltpu.make_async_copy(refs[i], refs[5 + i], sem.at[i]) for i in range(5)]
+    for copy in copies:
+        copy.start()
+    for copy in copies:
+        copy.wait()
+
+
 def packed_body(devices, projected, long_filter, short_kernel, skip_gain, cotangent):
     rows, channels = long_filter.shape
     span = short_kernel.shape[1]
@@ -419,6 +477,7 @@
     block = (devices, rows, LANES)
     pair = (devices, 2, rows, LANES)
     narrow, full = jnp.bfloat16, jnp.float32
+    arguments = (projected, cotangent, long_filter, short_kernel, skip_gain[None], *tables)
     in_vmem = pl.BlockSpec(memory_space=pltpu.VMEM)
     found = pl.pallas_call(
         functools.partial(layer_kernel, devices),
@@ -429,9 +488,10 @@
             jax.ShapeDtypeStruct(short_kernel.shape, full),
             jax.ShapeDtypeStruct((1, channels), full),
         ),
-        in_specs=[in_vmem] * 7,
+        in_specs=[pl.BlockSpec(memory_space=pltpu.HBM)] * 7,
         out_specs=(in_vmem,) * 5,
         scratch_shapes=[
+            *(pltpu.VMEM(value.shape, value.dtype) for value in arguments),
             pltpu.VMEM(pair, narrow),
             pltpu.VMEM(pair, narrow),
             pltpu.VMEM(block, narrow),
@@ -447,14 +507,23 @@
             pltpu.VMEM((extent, LANES), full),
             pltpu.VMEM((extent, LANES), full),
             pltpu.VMEM((extent, LANES), full),
-            pltpu.VMEM((slabs // 2 + 1, rows, 2 * LANES), full),
+            *[pltpu.VMEM((slabs // 2 + 1, rows, LANES), full)] * 3,
+            pltpu.SemaphoreType.DMA((len(arguments),)),
             pltpu.SemaphoreType.DMA((5, devices)),
             pltpu.SemaphoreType.DMA((5, devices)),
         ],
         compiler_params=pltpu.CompilerParams(
-            collective_id=0, has_side_effects=True, vmem_limit_bytes=40 * 1024 * 1024
+            collective_id=0, has_side_effects=True, vmem_limit_bytes=LIMIT
         ),
-    )(projected, long_filter, short_kernel, skip_gain[None], cotangent, *tables)
+    )(*arguments)
+    found = pl.pallas_call(
+        store_kernel,
+        out_shape=tuple(jax.ShapeDtypeStruct(value.shape, value.dtype) for value in found),
+        in_specs=[in_vmem] * 5,
+        out_specs=(pl.BlockSpec(memory_space=pltpu.HBM),) * 5,
+        scratch_shapes=[pltpu.SemaphoreType.DMA((5,))],
+        compiler_params=pltpu.CompilerParams(vmem_limit_bytes=LIMIT),
+    )(*found)
     return (*found[:4], found[4][0])
 
 

time: 57.4 us -> 48.2 us (0.84)
  local copies, waits for them, and re-layouts: 9.75 us -> 0 us
  Pallas kernels: 46.6 us -> 47.4 us
    unnamed x19 -> x0, local copies, waits for them, and re-layouts: 9.75 us -> none
    pallas_call x0 -> x1, Pallas kernels: none -> 2.08 us  [packed_body(): pl.pallas_call(store_kernel, out_shape=tuple((jax.ShapeDtypeStruct(value....]
    pallas_call x1, Pallas kernels: 46.6 us -> 45.3 us  [packed_body(): pl.pallas_call(functools.partial(layer_kernel, devices), out_shape=(jax.S...]
where the time goes in v2:
time: 48.2 us; the launch traced here: 48 us
  Pallas kernels  47.4 us (98%)
  between operations  0.64 us (1%)
    pallas_call x1, Pallas kernels, packed_body(): pl.pallas_call(functools.partial(layer_kernel, devices), out_shape=(jax.S...  45.3 us
    pallas_call x1, Pallas kernels, packed_body(): pl.pallas_call(store_kernel, out_shape=tuple((jax.ShapeDtypeStruct(value....  2.08 us

profile of v2, /device:TPU:0, one launch (start us, length us, event | category | flops | bytes accessed | tf_op | source)
XLA Modules:
  0.0 48.0 jit_solution(9880608747745101939)
XLA Ops:
  0.6 45.3 %shard_map.110 = (bf16[128,512]{1,0:T(8,128)(2,1)}, bf16[3,128,512]{2,1,0:T(8,128)(2,1)}, f32[128,512]{1,0:T(8,128)}, f32[3,7,512]{2,1,0:T(8,128)}, f32[1,512]{1,0:T(1,128)}) custom-call(bf16[3,128,512]{2,1,0:T(8,128)(2,1)} %projected_in.1, bf16[128,512]{1,0:T(8,128)(2,1)} %cotangent_in.1, f32[128,512]{1,0:T(8,128)} %filter_in.1, f32[3,7,512]{2,1,0:T(8,128)} %taps_in.1, ...), custom_call_target="tpu_custom_call" | custom-call | tf_op jit(solution)/shard_map/pallas_call | solution.py:482
  45.9 2.1 %shard_map.111 = (bf16[128,512]{1,0:T(8,128)(2,1)}, bf16[3,128,512]{2,1,0:T(8,128)(2,1)}, f32[128,512]{1,0:T(8,128)}, f32[3,7,512]{2,1,0:T(8,128)}, f32[1,512]{1,0:T(1,128)}) custom-call(bf16[128,512]{1,0:T(8,128)(2,1)} %get-tuple-element.15.refs_0_, bf16[3,128,512]{2,1,0:T(8,128)(2,1)} %get-tuple-element.16.refs_1_, f32[128,512]{1,0:T(8,128)} %get-tuple-element.17.refs_2_, ...), custom_call_target="tpu_custom_call" | custom-call | tf_op jit(solution)/shard_map/pallas_call | solution.py:519

commit v3 on v2

--- a/solution.py
+++ b/solution.py
@@ -114,11 +114,9 @@
     gain_in,
     forward_in,
     inverse_in,
-    output_ref,
-    streams_ref,
-    filter_grad_ref,
-    taps_grad_ref,
-    gain_grad_ref,
+    recv_response,
+    recv_grads,
+    recv_sums,
     projected_ref,
     cotangent_ref,
     filter_ref,
@@ -131,11 +129,8 @@
     send_filter,
     recv_filter,
     send_grads,
-    recv_grads,
     send_response,
-    recv_response,
     send_sums,
-    recv_sums,
     first_rim,
     second_rim,
     first_short,
@@ -145,9 +140,11 @@
     product_spectra,
     filter_spectra,
     load_sem,
+    keep_sem,
     send_sem,
     recv_sem,
 ):
+    hops = [(devices // 2 + (-1) ** i * ((i + 1) // 2)) for i in range(devices - 1)]
     arguments = (projected_in, cotangent_in, filter_in, taps_in, gain_in, forward_in, inverse_in)
     held = (
         projected_ref,
@@ -171,7 +168,6 @@
     slabs = 2 * devices
     extent = rows * devices
     factor = 1.0 / math.sqrt(extent)
-    tiles = devices // 2
     me = lax.axis_index("seq")
     odd = lax.rem(me, 2) == 1
 
@@ -207,38 +203,48 @@
         return lax.rem(me + devices - hop, devices)
 
     barrier = pltpu.get_barrier_semaphore()
-    for hop in range(1, devices):
+    for hop in hops:
         pl.semaphore_signal(
             barrier, inc=1, device_id={"seq": peer_at(hop)}, device_id_type=pl.DeviceIdType.MESH
         )
 
     loads[0].wait()
     loads[1].wait()
-    for tile in range(tiles):
-        lanes = slice(tile * LANES, (tile + 1) * LANES)
+    def lanes_of(peer):
+        return pl.ds(pl.multiple_of((peer // 2) * LANES, LANES), LANES)
+
+    def join_for(peer, first, second):
+        flip = lax.rem(peer, 2) == 1
+        return jnp.where(
+            low_lanes(first.shape),
+            jnp.where(flip, swap(first), first),
+            jnp.where(flip, second, swap(second)),
+        ).astype(jnp.bfloat16)
+
+    def pack_pairs(peer, target):
+        lanes = lanes_of(peer)
         gate, left, right = [wide(projected_ref[s, :, lanes]) for s in range(3)]
-        upstream = wide(cotangent_ref[:, lanes])
-        for parity in range(2):
-            send_pairs[2 * tile + parity, 0] = join(left, gate, parity).astype(jnp.bfloat16)
-            send_pairs[2 * tile + parity, 1] = join(right, upstream, parity).astype(jnp.bfloat16)
-    pl.semaphore_wait(barrier, devices - 1)
-    for hop in range(1, devices):
+        target[0] = join_for(peer, left, gate)
+        target[1] = join_for(peer, right, wide(cotangent_ref[:, lanes]))
+
+    def pack_filter(peer, target):
+        whole = filter_ref[:, lanes_of(peer)]
+        coarse = wide(whole.astype(jnp.bfloat16))
+        target[...] = join_for(peer, coarse, whole - coarse)
+
+    for place, hop in enumerate(hops):
         peer = peer_at(hop)
+        pack_pairs(peer, send_pairs.at[peer])
+        if place == 0:
+            pl.semaphore_wait(barrier, devices - 1)
         copy_to(0, hop, send_pairs.at[peer], recv_pairs, me, peer).start()
     loads[2].wait()
-    for tile in range(tiles):
-        lanes = slice(tile * LANES, (tile + 1) * LANES)
-        whole = filter_ref[:, lanes]
-        coarse = wide(whole.astype(jnp.bfloat16))
-        for parity in range(2):
-            send_filter[2 * tile + parity] = join(coarse, whole - coarse, parity).astype(
-                jnp.bfloat16
-            )
-    for hop in range(1, devices):
+    for hop in hops:
         peer = peer_at(hop)
+        pack_filter(peer, send_filter.at[peer])
         copy_to(1, hop, send_filter.at[peer], recv_filter, me, peer).start()
-    recv_pairs[me] = send_pairs[me]
-    recv_filter[me] = send_filter[me]
+    pack_pairs(me, recv_pairs.at[me])
+    pack_filter(me, recv_filter.at[me])
 
     for load in loads[3:5]:
         load.wait()
@@ -257,7 +263,7 @@
     gain = own_pair(own_gain, own_gain)
 
     def wait_from(kind, source, target):
-        for hop in range(1, devices):
+        for hop in hops:
             copy_to(kind, hop, source.at[peer_at(hop)], target, source_at(hop), peer_at(hop)).wait()
 
     def close_rim(rim):
@@ -343,10 +349,20 @@
         return carry
 
     lax.fori_loop(0, width // 16, filter_back, 0)
-    for hop in range(1, devices):
+    for hop in hops:
         peer = peer_at(hop)
         copy_to(2, hop, send_response.at[peer], recv_response, me, peer).start()
-    recv_response[me] = send_response[me]
+    kept = [
+        pltpu.make_async_copy(source, target.at[me], keep_sem.at[index])
+        for index, (source, target) in enumerate(
+            (
+                (send_response.at[me], recv_response),
+                (send_grads.at[me], recv_grads),
+                (send_sums, recv_sums),
+            )
+        )
+    ]
+    kept[0].start()
 
     wait_from(1, send_filter, recv_filter)
 
@@ -411,34 +427,64 @@
                 )
         return tuple(sums)
 
-    def step_grads(hop, sums):
+    def step_grads(step, sums):
+        hop = devices // 2 + (step + 1) // 2 * (1 - 2 * lax.rem(step, 2))
         peer = peer_at(hop)
         sums = grads(peer, sums)
         copy_to(3, hop, send_grads.at[peer], recv_grads, me, peer).start()
         return sums
 
     sums = tuple(jnp.zeros((8, LANES), jnp.float32) for _ in range(2 * span))
-    sums = lax.fori_loop(1, devices, step_grads, sums)
+    sums = lax.fori_loop(0, devices - 1, step_grads, sums)
     sums = grads(me, sums)
     for index, value in enumerate(sums + (gain_sum,)):
         send_sums[index : index + 1] = factor * jnp.sum(value, axis=0, keepdims=True)
-    for hop in range(1, devices):
+    for hop in hops:
         copy_to(4, hop, send_sums, recv_sums, me, peer_at(hop)).start()
-    recv_sums[me] = send_sums[...]
-    recv_grads[me] = send_grads[me]
+    kept[1].start()
+    kept[2].start()
+    for keep in kept:
+        keep.wait()
+    wait_from(2, send_response, recv_response)
+    wait_from(3, send_grads, recv_grads)
+    for hop in hops:
+        copy_to(4, hop, send_sums, recv_sums, source_at(hop), peer_at(hop)).wait()
+
+
+def unpack_kernel(*refs):
+    packed, results, held, refs = refs[:3], refs[3:8], refs[8:11], refs[11:]
+    output_ref, streams_ref, filter_grad_ref, taps_grad_ref, gain_grad_ref = refs[:5]
+    recv_response, recv_grads, recv_sums = held
+    load_sem, store_sem = refs[5:]
+    loads = [pltpu.make_async_copy(packed[i], held[i], load_sem.at[i]) for i in range(3)]
+    stores = [pltpu.make_async_copy(refs[i], results[i], store_sem.at[i]) for i in range(5)]
+    for load in loads:
+        load.start()
+    tiles = recv_response.shape[0] // 2
+    span = taps_grad_ref.shape[1]
+
+    def low_lanes(shape):
+        return lax.broadcasted_iota(jnp.int32, shape, 1) < HALF
+
+    def swap(value):
+        return pltpu.roll(value, HALF, 1)
+
+    def wide(value):
+        return value.astype(jnp.float32)
 
     def split(first, second):
         low = low_lanes(first.shape)
         return jnp.where(low, first, swap(second)), jnp.where(low, swap(first), second)
 
-    wait_from(2, send_response, recv_response)
+    loads[0].wait()
     for tile in range(tiles):
         lanes = slice(tile * LANES, (tile + 1) * LANES)
         first, second = wide(recv_response[2 * tile]), wide(recv_response[2 * tile + 1])
         filter_grad_ref[:, lanes] = jnp.where(
             low_lanes(first.shape), first + swap(first), second + swap(second)
         )
-    wait_from(3, send_grads, recv_grads)
+    stores[2].start()
+    loads[1].wait()
     for tile in range(tiles):
         lanes = slice(tile * LANES, (tile + 1) * LANES)
         for which, targets in enumerate(
@@ -447,8 +493,9 @@
             pieces = split(wide(recv_grads[2 * tile, which]), wide(recv_grads[2 * tile + 1, which]))
             for target, piece in zip(targets, pieces):
                 target[:, lanes] = piece.astype(jnp.bfloat16)
-    for hop in range(1, devices):
-        copy_to(4, hop, send_sums, recv_sums, source_at(hop), peer_at(hop)).wait()
+    stores[0].start()
+    stores[1].start()
+    loads[2].wait()
     for tile in range(tiles):
         lanes = slice(tile * LANES, (tile + 1) * LANES)
         low_part, high_part = split(recv_sums[2 * tile], recv_sums[2 * tile + 1])
@@ -456,15 +503,10 @@
         taps_grad_ref[0, :, lanes] = high_part[0:span]
         taps_grad_ref[2, :, lanes] = low_part[span : 2 * span]
         gain_grad_ref[:, lanes] = low_part[2 * span : 2 * span + 1]
-
-
-def store_kernel(*refs):
-    sem = refs[10]
-    copies = [pltpu.make_async_copy(refs[i], refs[5 + i], sem.at[i]) for i in range(5)]
-    for copy in copies:
-        copy.start()
-    for copy in copies:
-        copy.wait()
+    stores[3].start()
+    stores[4].start()
+    for store in stores:
+        store.wait()
 
 
 def packed_body(devices, projected, long_filter, short_kernel, skip_gain, cotangent):
@@ -478,18 +520,24 @@
     pair = (devices, 2, rows, LANES)
     narrow, full = jnp.bfloat16, jnp.float32
     arguments = (projected, cotangent, long_filter, short_kernel, skip_gain[None], *tables)
-    in_vmem = pl.BlockSpec(memory_space=pltpu.VMEM)
-    found = pl.pallas_call(
+    in_hbm = pl.BlockSpec(memory_space=pltpu.HBM)
+    packed_shapes = (
+        jax.ShapeDtypeStruct(block, narrow),
+        jax.ShapeDtypeStruct(pair, narrow),
+        jax.ShapeDtypeStruct((devices, sums_rows, LANES), full),
+    )
+    out_shapes = (
+        jax.ShapeDtypeStruct((rows, channels), narrow),
+        jax.ShapeDtypeStruct((3, rows, channels), narrow),
+        jax.ShapeDtypeStruct((rows, channels), full),
+        jax.ShapeDtypeStruct(short_kernel.shape, full),
+        jax.ShapeDtypeStruct((1, channels), full),
+    )
+    packed = pl.pallas_call(
         functools.partial(layer_kernel, devices),
-        out_shape=(
-            jax.ShapeDtypeStruct((rows, channels), narrow),
-            jax.ShapeDtypeStruct((3, rows, channels), narrow),
-            jax.ShapeDtypeStruct((rows, channels), full),
-            jax.ShapeDtypeStruct(short_kernel.shape, full),
-            jax.ShapeDtypeStruct((1, channels), full),
-        ),
-        in_specs=[pl.BlockSpec(memory_space=pltpu.HBM)] * 7,
-        out_specs=(in_vmem,) * 5,
+        out_shape=packed_shapes,
+        in_specs=[in_hbm] * 7,
+        out_specs=(in_hbm,) * 3,
         scratch_shapes=[
             *(pltpu.VMEM(value.shape, value.dtype) for value in arguments),
             pltpu.VMEM(pair, narrow),
@@ -497,11 +545,8 @@
             pltpu.VMEM(block, narrow),
             pltpu.VMEM(block, narrow),
             pltpu.VMEM(pair, narrow),
-            pltpu.VMEM(pair, narrow),
-            pltpu.VMEM(block, narrow),
             pltpu.VMEM(block, narrow),
             pltpu.VMEM((sums_rows, LANES), full),
-            pltpu.VMEM((devices, sums_rows, LANES), full),
             pltpu.VMEM((2, extent + 2 * RIM, LANES), full),
             pltpu.VMEM((2, extent + 2 * RIM, LANES), full),
             pltpu.VMEM((extent, LANES), full),
@@ -509,6 +554,7 @@
             pltpu.VMEM((extent, LANES), full),
             *[pltpu.VMEM((slabs // 2 + 1, rows, LANES), full)] * 3,
             pltpu.SemaphoreType.DMA((len(arguments),)),
+            pltpu.SemaphoreType.DMA((3,)),
             pltpu.SemaphoreType.DMA((5, devices)),
             pltpu.SemaphoreType.DMA((5, devices)),
         ],
@@ -517,13 +563,17 @@
         ),
     )(*arguments)
     found = pl.pallas_call(
-        store_kernel,
-        out_shape=tuple(jax.ShapeDtypeStruct(value.shape, value.dtype) for value in found),
-        in_specs=[in_vmem] * 5,
-        out_specs=(pl.BlockSpec(memory_space=pltpu.HBM),) * 5,
-        scratch_shapes=[pltpu.SemaphoreType.DMA((5,))],
+        unpack_kernel,
+        out_shape=out_shapes,
+        in_specs=[in_hbm] * 3,
+        out_specs=(in_hbm,) * 5,
+        scratch_shapes=[
+            *(pltpu.VMEM(value.shape, value.dtype) for value in packed_shapes + out_shapes),
+            pltpu.SemaphoreType.DMA((3,)),
+            pltpu.SemaphoreType.DMA((5,)),
+        ],
         compiler_params=pltpu.CompilerParams(vmem_limit_bytes=LIMIT),
-    )(*found)
+    )(*packed)
     return (*found[:4], found[4][0])
 
 

time: 48.2 us -> 46.6 us (0.967)
  Pallas kernels: 47.4 us -> 45.8 us
    pallas_call x2, Pallas kernels: 47.4 us -> 45.8 us  [the longest x1 43.6 us: packed_body(): pl.pallas_call(functools.partial(layer_kernel, devices), out_shape=packed...]
where the time goes in v3:
time: 46.6 us; the launch traced here: 46.4 us
  Pallas kernels  45.8 us (98%)
  between operations  0.64 us (1%)
    pallas_call x1, Pallas kernels, packed_body(): pl.pallas_call(functools.partial(layer_kernel, devices), out_shape=packed...  43.6 us
    pallas_call x1, Pallas kernels, packed_body(): pl.pallas_call(unpack_kernel, out_shape=out_shapes, in_specs=[in_hbm] * 3...  2.19 us

profile of v3, /device:TPU:0, one launch (start us, length us, event | category | flops | bytes accessed | tf_op | source)
XLA Modules:
  0.0 46.4 jit_solution(11284898903782656351)
XLA Ops:
  0.6 43.6 %shard_map.110 = (bf16[8,128,128]{2,1,0:T(8,128)(2,1)}, bf16[8,2,128,128]{3,2,1,0:T(8,128)(2,1)}, f32[8,16,128]{2,1,0:T(8,128)}) custom-call(bf16[3,128,512]{2,1,0:T(8,128)(2,1)} %projected_in.1, bf16[128,512]{1,0:T(8,128)(2,1)} %cotangent_in.1, f32[128,512]{1,0:T(8,128)} %filter_in.1, f32[3,7,512]{2,1,0:T(8,128)} %taps_in.1, f32[1,512]{1,0:T(1,128)} %bitcast.2, ...), custom_call_target="tpu_custom_call" | custom-call | tf_op jit(solution)/shard_map/pallas_call | solution.py:536
  44.2 2.2 %shard_map.111 = (bf16[128,512]{1,0:T(8,128)(2,1)}, bf16[3,128,512]{2,1,0:T(8,128)(2,1)}, f32[128,512]{1,0:T(8,128)}, f32[3,7,512]{2,1,0:T(8,128)}, f32[1,512]{1,0:T(1,128)}) custom-call(bf16[8,128,128]{2,1,0:T(8,128)(2,1)} %get-tuple-element.13.refs_0_, bf16[8,2,128,128]{3,2,1,0:T(8,128)(2,1)} %get-tuple-element.14.refs_1_, ...), custom_call_target="tpu_custom_call" | custom-call | tf_op jit(solution)/shard_map/pallas_call | solution.py:565

commit v4 on v3

--- a/solution.py
+++ b/solution.py
@@ -437,8 +437,12 @@
     sums = tuple(jnp.zeros((8, LANES), jnp.float32) for _ in range(2 * span))
     sums = lax.fori_loop(0, devices - 1, step_grads, sums)
     sums = grads(me, sums)
-    for index, value in enumerate(sums + (gain_sum,)):
-        send_sums[index : index + 1] = factor * jnp.sum(value, axis=0, keepdims=True)
+    sums = [factor * jnp.sum(value, axis=0, keepdims=True) for value in sums + (gain_sum,)]
+    middle = (span + 1) // 2
+    for index in range(span):
+        send_sums[index : index + 1] = sums[index]
+    for index in range(span, span + middle):
+        send_sums[index : index + 1] = join(sums[index], sums[index + middle], 0)
     for hop in hops:
         copy_to(4, hop, send_sums, recv_sums, me, peer_at(hop)).start()
     kept[1].start()
@@ -462,6 +466,7 @@
         load.start()
     tiles = recv_response.shape[0] // 2
     span = taps_grad_ref.shape[1]
+    middle = (span + 1) // 2
 
     def low_lanes(shape):
         return lax.broadcasted_iota(jnp.int32, shape, 1) < HALF
@@ -501,8 +506,9 @@
         low_part, high_part = split(recv_sums[2 * tile], recv_sums[2 * tile + 1])
         taps_grad_ref[1, :, lanes] = low_part[0:span]
         taps_grad_ref[0, :, lanes] = high_part[0:span]
-        taps_grad_ref[2, :, lanes] = low_part[span : 2 * span]
-        gain_grad_ref[:, lanes] = low_part[2 * span : 2 * span + 1]
+        taps_grad_ref[2, :middle, lanes] = low_part[span:]
+        taps_grad_ref[2, middle:, lanes] = high_part[span : 2 * span - middle]
+        gain_grad_ref[:, lanes] = high_part[2 * span - middle : 2 * span - middle + 1]
     stores[3].start()
     stores[4].start()
     for store in stores:
@@ -515,7 +521,7 @@
     extent = rows * devices
     slabs = 2 * devices
     tables = fine_tables(slabs, rows // 2)
-    sums_rows = -(-(2 * span + 1) // 8) * 8
+    sums_rows = span + (span + 1) // 2
     block = (devices, rows, LANES)
     pair = (devices, 2, rows, LANES)
     narrow, full = jnp.bfloat16, jnp.float32

time: 46.6 us -> 46.2 us (level)
  no operation moved by 1% of the time
where the time goes in v4:
time: 46.2 us; the launch traced here: 46 us
  Pallas kernels  45.4 us (98%)
  between operations  0.64 us (1%)
    pallas_call x1, Pallas kernels, packed_body(): pl.pallas_call(functools.partial(layer_kernel, devices), out_shape=packed...  43.2 us
    pallas_call x1, Pallas kernels, packed_body(): pl.pallas_call(unpack_kernel, out_shape=out_shapes, in_specs=[in_hbm] * 3...  2.19 us

profile of v4, /device:TPU:0, one launch (start us, length us, event | category | flops | bytes accessed | tf_op | source)
XLA Modules:
  0.0 46.0 jit_solution(17394518065457948382)
XLA Ops:
  0.6 43.2 %shard_map.110 = (bf16[8,128,128]{2,1,0:T(8,128)(2,1)}, bf16[8,2,128,128]{3,2,1,0:T(8,128)(2,1)}, f32[8,11,128]{2,1,0:T(8,128)}) custom-call(bf16[3,128,512]{2,1,0:T(8,128)(2,1)} %projected_in.1, bf16[128,512]{1,0:T(8,128)(2,1)} %cotangent_in.1, f32[128,512]{1,0:T(8,128)} %filter_in.1, f32[3,7,512]{2,1,0:T(8,128)} %taps_in.1, f32[1,512]{1,0:T(1,128)} %bitcast.2, ...), custom_call_target="tpu_custom_call" | custom-call | tf_op jit(solution)/shard_map/pallas_call | solution.py:542
  43.8 2.2 %shard_map.111 = (bf16[128,512]{1,0:T(8,128)(2,1)}, bf16[3,128,512]{2,1,0:T(8,128)(2,1)}, f32[128,512]{1,0:T(8,128)}, f32[3,7,512]{2,1,0:T(8,128)}, f32[1,512]{1,0:T(1,128)}) custom-call(bf16[8,128,128]{2,1,0:T(8,128)(2,1)} %get-tuple-element.13.refs_0_, bf16[8,2,128,128]{3,2,1,0:T(8,128)(2,1)} %get-tuple-element.14.refs_1_, ...), custom_call_target="tpu_custom_call" | custom-call | tf_op jit(solution)/shard_map/pallas_call | solution.py:571
